TPU v7x, 256 devices: a whole 4x4x8 slice. The times are simulated.
256 devices in a mesh: section: 2 (over core), dp: 8 (over y, z_lo), tensor: 16 (over x, z_hi).
Axes of the slice: x: 4, y: 4, z: 8 (z_hi: 4, z_lo: 2; z = z_hi * 2 + z_lo), core: 2. Of those that a mesh axis runs over, the one named last changes fastest.
Arguments:
- residual_parts: bfloat16 [2, 3072, 16384], P('section', 'dp', 'tensor'), may hold values from -120 to 120
- attn_out: bfloat16 [2, 3072, 16384], P('section', 'dp', 'tensor'), may hold values from -6 to 6
- ffn_input: bfloat16 [2, 3072, 53248], P('section', 'dp', 'tensor'), may hold values from -6 to 6
- norm_gain: float32 [2, 16384], P('section', 'tensor'), may hold values from 0.25 to 1.75
- mixing: bfloat16 [2, 52, 52], P('section'), may hold values from -0.875 to 0.875
- blocks: int32 [2, 2], P('section'), may hold values from 0 to 25, as said below
Outputs:
- hess_in: float32 [2, 16384, 1024], P('section', 'tensor', 'dp')
- hess_o: float32 [2, 16384, 1024], P('section', 'tensor', 'dp')
- hess_down: float32 [2, 2048, 2048], P('section', 'tensor', 'dp')
Inputs may be any that keep to these rules, and one draw needn't show every extreme that they name: `blocks`: entry [s, 0] is below 16; entry [s, 1] is below 26. In every draw one layer has entry [s, 0] = 0 and entry [s, 1] = 25.
All inputs are finite; a program needn't handle non-finite values.
Results may differ from a plain program's by a relative error of at most 0.0038.
Values may be sent and summed in bfloat16 or wider, within the bound.
No kernel may reach another device: no remote copies, remote signals or barrier semaphores. Data moves between devices by JAX's collectives and lax.ppermute only.
A program may use at most 64 MiB of HBM per device.

v0:
```python
import math
import jax
import jax.numpy as jnp
from jax import lax
from jax.sharding import Mesh
from jax.sharding import PartitionSpec as P

D = 16384
KB = 52
HBLK = 1024
BLK = 2048
TENSOR = ("tensor_0", "tensor_1")
EPS = 1e-05


def passed_along(x, axis, by):
    devices = lax.axis_size(axis)
    pairs = [(i, i + by) for i in range(devices) if 0 <= i + by < devices]
    return lax.ppermute(x, axis, pairs)


def copy_for_each(x, axis):
    devices = lax.axis_size(axis)
    return lax.all_to_all(jnp.broadcast_to(x[None], (devices, *x.shape)), axis, 0, 0, tiled=True)


def over_copies(x, axis):
    everything = copy_for_each(x, axis)
    return jnp.sum(everything, axis=0)


def broadcast_by_axis(x, axes, root):
    x = jnp.where(lax.axis_index(axes) == root, x, jnp.zeros_like(x))
    for axis in axes:
        x = lax.psum(x, axis)
    return x


def in_blocks(x, dim, devices):
    before, after = (x.shape[:dim], x.shape[dim + 1 :])
    return jnp.moveaxis(x.reshape(*before, devices, -1, *after), dim, 0)


def summed_on_arrival(x, axis, dim):
    tiles = in_blocks(x, dim, lax.axis_size(axis))
    arrived = lax.all_to_all(tiles, axis, split_axis=0, concat_axis=0, tiled=True)
    return arrived.sum(axis=0)


def in_one_piece(arrays, axis, dim, along):
    both = jnp.concatenate(arrays, axis=along)
    out, at, done = (lax.psum_scatter(both, axis, scatter_dimension=dim, tiled=True), 0, [])
    for a in arrays:
        done.append(lax.slice_in_dim(out, at, at + a.shape[along], axis=along))
        at += a.shape[along]
    return tuple(done)


def bit_parity(values):
    total = jnp.zeros_like(values)
    for position in range(16):
        total = total + values // (1 << position) % 2
    return total % 2


def sylvester(order):
    index = jnp.arange(order, dtype=jnp.int32)
    parity = bit_parity(jnp.bitwise_and(index[:, None], index[None, :]))
    return (1 - 2 * parity).astype(jnp.float32)


def gram(left, right):
    return lax.dot_general(
        left, right, (((0,), (0,)), ((), ())), preferred_element_type=jnp.float32
    )


def local(residual_parts, attn_out, ffn_input, norm_gain, mixing, blocks):
    local_d = residual_parts.shape[2]
    local_f = ffn_input.shape[2]
    token_rows = residual_parts.shape[1]
    own_part = residual_parts[0]
    earlier = passed_along(own_part, "section", 1)
    layer_in = earlier.astype(jnp.float32) + own_part.astype(jnp.float32)
    square_total = over_copies(jnp.sum(layer_in * layer_in, axis=1), TENSOR)
    normed = (layer_in * lax.rsqrt(square_total / D + EPS)[:, None] * norm_gain[0][None, :]).astype(
        jnp.bfloat16
    )
    attention = attn_out[0]
    first_col = blocks[0, 0] * HBLK
    norm_list, attn_list = ([], [])
    owner = first_col // local_d + 0
    norm_got = broadcast_by_axis(normed, TENSOR, owner)
    attn_got = broadcast_by_axis(attention, TENSOR, owner)
    norm_list.append(norm_got)
    attn_list.append(attn_got)
    norm_block = norm_list[0]
    attn_block = attn_list[0]
    tensor_count = lax.axis_size(TENSOR)
    member = lax.axis_index(TENSOR)
    a_local = local_f // KB
    order_a = a_local * tensor_count
    cube = ffn_input[0].reshape(token_rows, a_local, KB)
    mixed = jnp.einsum("rak,kc->rac", cube, mixing[0], preferred_element_type=jnp.float32)
    turned = jnp.einsum("rac,ae->rec", mixed, sylvester(a_local), precision=lax.Precision.HIGHEST)
    turned = turned.reshape(token_rows, local_f)
    start = blocks[0, 1] * BLK
    doubled = jnp.concatenate([turned, turned], axis=1)
    window = lax.dynamic_slice_in_dim(doubled, start % local_f, BLK, 1)
    target = (start + jnp.arange(BLK, dtype=jnp.int32)) // local_f
    parity = bit_parity(jnp.bitwise_and(target, member))
    signs = (1 - 2 * parity).astype(jnp.float32) / math.sqrt(order_a)
    term = window * signs[None, :]
    own_cols = summed_on_arrival(term, TENSOR, 1).astype(jnp.bfloat16)
    rotated = lax.all_gather(own_cols, TENSOR, axis=1, tiled=True)
    part_in = gram(normed, norm_block)
    part_o = gram(attention, attn_block)
    part_down = gram(own_cols, rotated)
    summed = (
        *in_one_piece((part_in, part_o), "dp", 1, 0),
        lax.psum_scatter(part_down, "dp", scatter_dimension=1, tiled=True),
    )
    scale = 2.0 / (token_rows * lax.axis_size("dp"))
    hess_in = (scale * summed[0])[None]
    hess_o = (scale * summed[1])[None]
    hess_down = (scale * summed[2])[None]
    return (hess_in, hess_o, hess_down)


def solution(mesh):
    finer = Mesh(
        mesh.devices.reshape(mesh.shape["section"], mesh.shape["dp"], 4, 4),
        ("section", "dp", "tensor_0", "tensor_1"),
    )
    in_specs = (
        P("section", "dp", TENSOR),
        P("section", "dp", TENSOR),
        P("section", "dp", TENSOR),
        P("section", TENSOR),
        P("section", None, None),
        P("section", None),
    )
    out_specs = (P("section", TENSOR, "dp"), P("section", TENSOR, "dp"), P("section", TENSOR, "dp"))
    return jax.shard_map(local, mesh=finer, in_specs=in_specs, out_specs=out_specs, check_vma=False)
```

profile of v0, /device:TPU:1, one launch (start us, length us, event | category | flops | bytes accessed | tf_op | source)
XLA Modules:
  0.0 455.9 jit_solution(6343559055614895578)
XLA Ops:
  8.0 0.0 copy-start
  8.0 1.3 collective-permute-start
  9.3 4.4 copy.20
  13.7 3.4 reshape_squeeze.3
  17.1 0.0 copy-done
  17.1 0.0 copy-start.9
  17.1 3.3 fusion.156
  20.4 0.0 copy-done.9
  20.4 0.6 fusion.253
  21.7 8.3 %fusion.4 = f32[384,64,52]{0,1,2:T(8,128)S(1)} fusion(f32[384,64,52]{0,2,1:T(8,128)} %fusion.156), kind=kOutput, calls=%fused_computation.7 | convolution fusion | flops 982917120 | bytes 10223616 | tf_op jit(solution)/shard_map/rac,ae->rec/dot_general | solution.py:105
  30.0 5.4 %copy.23 = f32[384,64,52]{0,2,1:T(8,128)} copy(f32[384,64,52]{0,1,2:T(8,128)S(1)} %fusion.4) | data formatting | bytes 10223616 | tf_op jit(solution)/shard_map/rac,ae->rec/transpose | solution.py:105
  35.4 0.0 copy-start.1
  35.4 6.4 %reshape.401 = f32[384,3328]{0,1:T(8,128)} reshape(f32[384,64,52]{0,2,1:T(8,128)} %copy.23) | data formatting | bytes 10223616 | tf_op jit(solution)/shard_map/reshape | solution.py:106
  41.7 0.1 fusion.207
  41.9 0.0 collective-permute-done
  41.9 0.0 copy-done.1
  41.9 0.0 copy-start.3
  41.9 0.3 multiply_reduce_fusion
  42.2 0.6 broadcast_in_dim.8
  42.8 11.6 %all-to-all-start = ((f32[16,1,384]{2,1,0:T(1,128)}), f32[16,1,384]{2,1,0:T(1,128)S(1)}, u32[]{:S(2)}, u32[]{:S(2)}) async-start(f32[16,1,384]{2,1,0:T(1,128)} %broadcast_in_dim.8), calls=%async_computation | async-start | bytes 49152 | tf_op jit(solution)/shard_map/all_to_all | solution.py:24
  54.5 4.5 fusion.3
  59.0 0.0 copy-done.3
  59.0 4.3 all-to-all-done
  63.3 0.0 copy-start.8
  63.3 0.0 copy-start.7
  63.3 0.6 copy-done.8
  63.9 4.7 %all-to-all-start.1 = ((f32[16,384,128]{1,2,0:T(8,128)}), f32[16,384,128]{1,2,0:T(8,128)S(1)}, u32[]{:S(2)}, u32[]{:S(2)}) async-start(f32[16,384,128]{1,2,0:T(8,128)} %bitcast.13), calls=%async_computation.2 | async-start | bytes 6291456 | tf_op jit(solution)/shard_map/all_to_all | solution.py:46
  68.6 0.0 all-reduce.7.cloned.1.call-start
  69.3 2.1 bitcast_select_fusion
  71.4 0.8 reduce_sum.28
  72.2 0.0 copy-done.7
  72.2 2.6 broadcast_select_fusion
  74.8 0.0 all-reduce.7.cloned.1.call-update
  74.9 0.0 all-gather.2.cloned.1.call-start
  74.9 62.6 %all-to-all-done.1 = f32[16,384,128]{1,2,0:T(8,128)S(1)} async-done(((f32[16,384,128]{1,2,0:T(8,128)}), f32[16,384,128]{1,2,0:T(8,128)S(1)}, u32[]{:S(2)}, u32[]{:S(2)}) %all-to-all-start.1) | async-done | bytes 3145760 | tf_op jit(solution)/shard_map/all_to_all | solution.py:46
  137.5 0.8 reduce_sum.29
  138.3 0.0 copy-start.5
  138.3 0.0 all-gather.2.cloned.1.call-update
  138.4 0.0 all-reduce.5.cloned.1.call-start
  138.4 15.9 %all-reduce.7.cloned.1.call-done = (bf16[384,1024]{1,0:T(8,128)(2,1)}, bf16[384,1024]{1,0:T(8,128)(2,1)}) async-done(((bf16[384,1024]{1,0:T(8,128)(2,1)}, bf16[384,1024]{1,0:T(8,128)(2,1)}), (bf16[384,1024]{1,0:T(8,128)(2,1)}, bf16[384,1024]{1,0:T(8,128)(2,1)})) %all-reduce.7.cloned.1.call-update) | async-done | bytes 1572880 | tf_op jit(solution)/shard_map/psum | solution.py:35
  154.3 0.0 all-reduce.5.cloned.1.call-update
  154.4 0.0 reduce-scatter.5.cloned.1.call-start
  154.4 56.3 %all-gather.2.cloned.1.call-done = bf16[384,2048]{0,1:T(8,128)(2,1)} async-done(((bf16[384,128]{0,1:T(8,128)(2,1)}), bf16[384,2048]{0,1:T(8,128)(2,1)}) %all-gather.2.cloned.1.call-update) | async-done | bytes 1572880 | tf_op jit(solution)/shard_map/all_gather | solution.py:115
  210.7 3.1 fusion.254
  213.8 0.0 reduce-scatter.5.cloned.1.call-update
  213.8 0.0 reduce-scatter.3.cloned.1.call-start
  213.9 41.1 %all-reduce.5.cloned.1.call-done = (bf16[384,1024]{1,0:T(8,128)(2,1)}, bf16[384,1024]{1,0:T(8,128)(2,1)}) async-done(((bf16[384,1024]{1,0:T(8,128)(2,1)}, bf16[384,1024]{1,0:T(8,128)(2,1)}), (bf16[384,1024]{1,0:T(8,128)(2,1)}, bf16[384,1024]{1,0:T(8,128)(2,1)})) %all-reduce.5.cloned.1.call-update) | async-done | bytes 1572880 | tf_op jit(solution)/shard_map/psum | solution.py:35
  255.0 0.0 copy-done.5
  255.0 0.0 copy-start.2
  255.0 0.0 copy-start.4
  255.0 0.0 copy-start.6
  255.0 2.6 convolution_bitcast_fusion
  257.6 0.0 copy-done.2
  257.6 0.0 copy-done.4
  257.7 0.0 copy-done.6
  257.7 1.4 fusion.252
  259.1 4.1 pad_maximum_fusion
  263.2 0.0 reduce-scatter.3.cloned.1.call-update
  263.2 6.4 %reduce-scatter.5.cloned.1.call-done = f32[128,256]{1,0:T(8,128)} async-done(((f32[128,2048]{1,0:T(8,128)}), f32[128,256]{1,0:T(8,128)}) %reduce-scatter.5.cloned.1.call-update) | async-done | bytes 131088 | tf_op jit(solution)/shard_map/reduce_scatter | solution.py:121
  269.6 1.6 multiply_bitcast_fusion
  271.1 174.9 %reduce-scatter.3.cloned.1.call-done = f32[2048,128]{1,0:T(8,128)} async-done(((f32[2048,1024]{1,0:T(8,128)}), f32[2048,128]{1,0:T(8,128)}) %reduce-scatter.3.cloned.1.call-update) | async-done | bytes 1048592 | tf_op jit(solution)/shard_map/reduce_scatter | solution.py:52
  446.1 2.3 fusion.8
  (1 shorter events, 0.0 us)
Async XLA Ops:
  8.0 9.1 %copy-start = (bf16[1,52,52]{2,1,0:T(8,128)(2,1)S(1)}, bf16[1,52,52]{2,1,0:T(8,128)(2,1)}, u32[]{:S(2)}) copy-start(bf16[1,52,52]{2,1,0:T(8,128)(2,1)} %param.10) | copy-start | bytes 16228
  8.0 33.8 %collective-permute-start = (bf16[384,1024]{1,0:T(8,128)(2,1)}, bf16[384,1024]{1,0:T(8,128)(2,1)S(1)}, u32[]{:S(2)}, u32[]{:S(2)}) collective-permute-start(bf16[384,1024]{1,0:T(8,128)(2,1)} %bitcast.43), channel_id=1, source_target_pairs={{0,128},{1,129},{2,130},{3,131},{4,132},{5,133},{6,134},{7,135},{8... | collective-permute-start | bytes 2359304 | tf_op jit(solution)/shard_map/ppermute | solution.py:19
  17.1 3.3 copy-start.9
  35.4 6.5 %copy-start.1 = (bf16[1,384,1024]{2,1,0:T(8,128)(2,1)S(1)}, bf16[1,384,1024]{2,1,0:T(8,128)(2,1)}, u32[]{:S(2)}) copy-start(bf16[1,384,1024]{2,1,0:T(8,128)(2,1)} %param.6) | copy-start | bytes 2359300
  41.9 17.1 %copy-start.3 = (bf16[384,1024]{1,0:T(8,128)(2,1)}, bf16[384,1024]{1,0:T(8,128)(2,1)S(1)}, u32[]{:S(2)}) copy-start(bf16[384,1024]{1,0:T(8,128)(2,1)S(1)} %collective-permute-done) | copy-start | bytes 2359300
  42.8 20.4 %all-to-all-start = ((f32[16,1,384]{2,1,0:T(1,128)}), f32[16,1,384]{2,1,0:T(1,128)S(1)}, u32[]{:S(2)}, u32[]{:S(2)}) async-start(f32[16,1,384]{2,1,0:T(1,128)} %broadcast_in_dim.8), calls=%async_computation | async-start | bytes 49152 | tf_op jit(solution)/shard_map/all_to_all | solution.py:24
  63.3 0.6 copy-start.8
  63.3 8.9 %copy-start.7 = (f32[1,1024]{1,0:T(1,128)S(1)}, f32[1,1024]{1,0:T(1,128)}, u32[]{:S(2)}) copy-start(f32[1,1024]{1,0:T(1,128)} %param.9) | copy-start | bytes 12292
  63.9 73.6 %all-to-all-start.1 = ((f32[16,384,128]{1,2,0:T(8,128)}), f32[16,384,128]{1,2,0:T(8,128)S(1)}, u32[]{:S(2)}, u32[]{:S(2)}) async-start(f32[16,384,128]{1,2,0:T(8,128)} %bitcast.13), calls=%async_computation.2 | async-start | bytes 6291456 | tf_op jit(solution)/shard_map/all_to_all | solution.py:46
  68.6 85.7 %all-reduce.7.cloned.1.call-start = ((), (), s32[]{:S(2)}) async-start(), calls=%async_computation.8 | async-start | bytes 3145728 | tf_op jit(solution)/shard_map/psum | solution.py:35
  74.9 135.8 %all-gather.2.cloned.1.call-start = ((), (), s32[]{:S(2)}) async-start(), calls=%async_computation.5 | async-start | bytes 1671168 | tf_op jit(solution)/shard_map/all_gather | solution.py:115
  138.3 116.7 %copy-start.5 = (bf16[1,384,1024]{2,1,0:T(8,128)(2,1)S(1)}, bf16[1,384,1024]{2,1,0:T(8,128)(2,1)}, u32[]{:S(2)}) copy-start(bf16[1,384,1024]{2,1,0:T(8,128)(2,1)} %param.7) | copy-start | bytes 2359300
  138.4 116.7 %all-reduce.5.cloned.1.call-start = ((), (), s32[]{:S(2)}) async-start(), calls=%async_computation.7 | async-start | bytes 3145728 | tf_op jit(solution)/shard_map/psum | solution.py:35
  154.4 115.2 %reduce-scatter.5.cloned.1.call-start = ((), (), s32[]{:S(2)}) async-start(), calls=%async_computation.6 | async-start | bytes 1179648 | tf_op jit(solution)/shard_map/reduce_scatter | solution.py:121
  213.8 232.2 %reduce-scatter.3.cloned.1.call-start = ((), (), s32[]{:S(2)}) async-start(), calls=%async_computation.4 | async-start | bytes 9437184 | tf_op jit(solution)/shard_map/reduce_scatter | solution.py:52
  255.0 2.6 copy-start.2
  255.0 2.6 copy-start.4
  255.0 2.6 copy-start.6
Sparse Core Ops, SparseCore 0:
  75.0 79.3 all-reduce.6
  157.0 97.9 all-reduce.4
Sparse Core Ops, SparseCore 1:
  138.4 72.2 all-gather.1
  213.9 55.6 reduce-scatter.4
  272.0 174.0 reduce-scatter.2
where the time goes:
time: 457 us; the launch traced here: 456 us
  waiting for transfers between devices  362 us (79%)
  local copies, waits for them, and re-layouts  21.4 us (5%)
  other arithmetic  19.1 us (4%)
  matrix products  18.8 us (4%)
  starting transfers between devices  17.8 us (4%)
  between operations  17.2 us (4%)
    reduce_scatter x1, waiting for transfers between devices, in_one_piece(): lax.psum_scatter(both, axis, scatter_dimension=dim, tiled=True)  175 us
    all_to_all x1, waiting for transfers between devices, summed_on_arrival(): lax.all_to_all(tiles, axis, split_axis=0, concat_axis=0, tiled=True)  62.6 us
    psum x2, waiting for transfers between devices, broadcast_by_axis(): x = lax.psum(x, axis)  57.1 us
    all_gather x1, waiting for transfers between devices, local(): rotated = lax.all_gather(own_cols, TENSOR, axis=1, tiled=True)  56.3 us
    all_to_all x1, starting transfers between devices, copy_for_each(): lax.all_to_all(jnp.broadcast_to(x[None], (devices, *x.shape)), axis, 0, 0...  11.6 us
  transfers between devices with their start and end apart: 8, of which 7 were waited for; matrix products, arithmetic and copies ran while one was open for 12% of the time, Pallas kernels for 0%

commit v1 on v0

--- a/solution.py
+++ b/solution.py
@@ -11,6 +11,12 @@
 BLK = 2048
 TENSOR = ("tensor_0", "tensor_1")
 EPS = 1e-05
+
+
+def _carry_shapes(in_array, row_axis):
+    v_now = jax.lax.all_gather(in_array, row_axis)
+    side_arr = jnp.sum(v_now, axis=0)
+    return side_arr
 
 
 def passed_along(x, axis, by):
@@ -32,7 +38,7 @@
 def broadcast_by_axis(x, axes, root):
     x = jnp.where(lax.axis_index(axes) == root, x, jnp.zeros_like(x))
     for axis in axes:
-        x = lax.psum(x, axis)
+        x = _carry_shapes(x, axis)
     return x
 
 

time: 457 us -> 567 us (1.24)
  waiting for transfers between devices: 362 us -> 459 us
  other arithmetic: 19.1 us -> 31.7 us
    all_gather x0 -> x4, waiting for transfers between devices: none -> 124 us  [_carry_shapes(): v_now = jax.lax.all_gather(in_array, row_axis)]
    psum x2 -> x0, waiting for transfers between devices: 57.1 us -> none  [broadcast_by_axis(): x = lax.psum(x, axis)]
    reduce_scatter x1, waiting for transfers between devices: 6.36 us -> 36.9 us  [local(): lax.psum_scatter(part_down, 'dp', scatter_dimension=1, tiled=True)]
    reduce_sum x0 -> x4, other arithmetic: none -> 12.4 us  [_carry_shapes(): side_arr = jnp.sum(v_now, axis=0)]
  transfers between devices with their start and end apart: 8 -> 10, of which waited for: 7 -> 7; matrix products, arithmetic and copies ran while one was open for 12% -> 12% of each run, Pallas kernels for 0% -> 0%
where the time goes in v1:
time: 567 us; the launch traced here: 566 us
  waiting for transfers between devices  459 us (81%)
  other arithmetic  31.7 us (6%)
  local copies, waits for them, and re-layouts  23 us (4%)
  matrix products  19.6 us (3%)
  starting transfers between devices  17 us (3%)
  between operations  15.7 us (3%)
    reduce_scatter x1, waiting for transfers between devices, in_one_piece(): lax.psum_scatter(both, axis, scatter_dimension=dim, tiled=True)  176 us
    all_gather x4, waiting for transfers between devices, _carry_shapes(): v_now = jax.lax.all_gather(in_array, row_axis)  124 us
    all_to_all x1, waiting for transfers between devices, summed_on_arrival(): lax.all_to_all(tiles, axis, split_axis=0, concat_axis=0, tiled=True)  61.8 us
    all_gather x1, waiting for transfers between devices, local(): rotated = lax.all_gather(own_cols, TENSOR, axis=1, tiled=True)  56.1 us
    reduce_scatter x1, waiting for transfers between devices, local(): lax.psum_scatter(part_down, 'dp', scatter_dimension=1, tiled=True)  36.9 us
    reduce_sum x4, other arithmetic, _carry_shapes(): side_arr = jnp.sum(v_now, axis=0)  12.4 us
  transfers between devices with their start and end apart: 10, of which 7 were waited for; matrix products, arithmetic and copies ran while one was open for 12% of the time, Pallas kernels for 0%

profile of v1, /device:TPU:1, one launch (start us, length us, event | category | flops | bytes accessed | tf_op | source)
XLA Modules:
  0.0 566.0 jit_solution(6381758772579402188)
XLA Ops:
  7.2 0.0 copy-start
  7.2 0.0 all-gather.9.cloned.1.call-start
  7.2 1.3 fusion.253
  9.2 2.1 broadcast_select_fusion
  11.3 0.0 all-gather.9.cloned.1.call-update
  11.3 1.3 collective-permute-start
  12.6 4.4 copy.20
  17.0 3.4 reshape_squeeze.3
  20.4 0.0 copy-done
  20.5 3.3 fusion.156
  24.5 8.4 %fusion.4 = f32[384,64,52]{0,1,2:T(8,128)S(1)} fusion(f32[384,64,52]{0,2,1:T(8,128)} %fusion.156), kind=kOutput, calls=%fused_computation.7 | convolution fusion | flops 982917120 | bytes 10223616 | tf_op jit(solution)/shard_map/rac,ae->rec/dot_general | solution.py:111
  32.9 5.4 copy.23
  38.3 6.4 %reshape.401 = f32[384,3328]{0,1:T(8,128)} reshape(f32[384,64,52]{0,2,1:T(8,128)} %copy.23) | data formatting | bytes 10223616 | tf_op jit(solution)/shard_map/reshape | solution.py:112
  44.7 0.1 fusion.207
  44.8 0.0 collective-permute-done
  44.8 0.0 copy-done.3
  44.8 0.0 copy-start.5
  44.8 0.3 multiply_reduce_fusion
  45.2 0.6 broadcast_in_dim.8
  45.8 10.7 %all-to-all-start = ((f32[16,1,384]{2,1,0:T(1,128)}), f32[16,1,384]{2,1,0:T(1,128)S(1)}, u32[]{:S(2)}, u32[]{:S(2)}) async-start(f32[16,1,384]{2,1,0:T(1,128)} %broadcast_in_dim.8), calls=%async_computation | async-start | bytes 49152 | tf_op jit(solution)/shard_map/all_to_all | solution.py:30
  56.5 4.5 fusion.3
  61.0 0.0 copy-done.5
  61.0 4.3 all-to-all-done
  65.4 0.6 copy-done.10
  66.0 4.7 all-to-all-start.1
  70.7 0.0 all-gather.13.cloned.1.call-start
  70.8 0.8 reduce_sum.76
  71.6 0.0 copy-done.9
  71.6 2.7 broadcast_select_fusion.1
  74.2 0.0 all-gather.13.cloned.1.call-update
  74.2 0.0 all-gather.11.cloned.1.call-start
  74.3 61.8 %all-to-all-done.1 = f32[16,384,128]{1,2,0:T(8,128)S(1)} async-done(((f32[16,384,128]{1,2,0:T(8,128)}), f32[16,384,128]{1,2,0:T(8,128)S(1)}, u32[]{:S(2)}, u32[]{:S(2)}) %all-to-all-start.1) | async-done | bytes 3145760 | tf_op jit(solution)/shard_map/all_to_all | solution.py:52
  136.1 0.8 reduce_sum.81
  136.9 0.0 all-gather.11.cloned.1.call-update
  136.9 0.0 all-gather.17.cloned.1.call-start
  137.0 0.0 all-gather.9.cloned.1.call-done
  137.0 3.6 reduce_sum.79
  140.6 0.0 all-gather.17.cloned.1.call-update
  140.7 0.0 all-gather.15.cloned.1.call-start
  140.7 0.0 all-gather.13.cloned.1.call-done
  140.7 3.6 reduce_sum.77
  144.4 0.0 all-gather.15.cloned.1.call-update
  144.4 0.0 reduce-scatter.5.cloned.1.call-start
  144.4 56.1 %all-gather.11.cloned.1.call-done = bf16[384,2048]{0,1:T(8,128)(2,1)} async-done(((bf16[384,128]{0,1:T(8,128)(2,1)}), bf16[384,2048]{0,1:T(8,128)(2,1)}) %all-gather.11.cloned.1.call-update) | async-done | bytes 1572880 | tf_op jit(solution)/shard_map/all_gather | solution.py:121
  200.6 0.0 copy-done.8
  200.6 3.0 fusion.254
  203.6 0.0 reduce-scatter.5.cloned.1.call-update
  203.6 0.0 reduce-scatter.3.cloned.1.call-start
  203.7 60.8 %all-gather.17.cloned.1.call-done = bf16[1536,1024]{1,0:T(8,128)(2,1)} async-done(((bf16[384,1024]{1,0:T(8,128)(2,1)}), bf16[1536,1024]{1,0:T(8,128)(2,1)}) %all-gather.17.cloned.1.call-update) | async-done | bytes 3145744 | tf_op jit(solution)/shard_map/all_gather | solution.py:17
  264.5 2.6 reduce_sum.80
  267.1 0.0 copy-done.7
  267.1 3.4 convolution_bitcast_fusion
  270.5 63.0 %all-gather.15.cloned.1.call-done = bf16[1536,1024]{1,0:T(8,128)(2,1)} async-done(((bf16[384,1024]{1,0:T(8,128)(2,1)}), bf16[1536,1024]{1,0:T(8,128)(2,1)}) %all-gather.15.cloned.1.call-update) | async-done | bytes 3145744 | tf_op jit(solution)/shard_map/all_gather | solution.py:17
  333.5 2.6 reduce_sum.78
  336.1 1.4 fusion.252
  337.5 0.8 copy-done.2
  338.3 4.2 pad_maximum_fusion
  342.5 0.0 reduce-scatter.3.cloned.1.call-update
  342.5 0.0 copy-start.1
  342.5 36.9 %reduce-scatter.5.cloned.1.call-done = f32[128,256]{1,0:T(8,128)} async-done(((f32[128,2048]{1,0:T(8,128)}), f32[128,256]{1,0:T(8,128)}) %reduce-scatter.5.cloned.1.call-update) | async-done | bytes 131088 | tf_op jit(solution)/shard_map/reduce_scatter | solution.py:127
  379.4 1.6 multiply_bitcast_fusion
  381.0 175.8 %reduce-scatter.3.cloned.1.call-done = f32[2048,128]{1,0:T(8,128)} async-done(((f32[2048,1024]{1,0:T(8,128)}), f32[2048,128]{1,0:T(8,128)}) %reduce-scatter.3.cloned.1.call-update) | async-done | bytes 1048592 | tf_op jit(solution)/shard_map/reduce_scatter | solution.py:58
  556.9 2.3 fusion.8
  559.1 0.0 copy-done.1
  (11 shorter events, 0.0 us)
Async XLA Ops:
  7.2 13.3 %copy-start = (bf16[1,52,52]{2,1,0:T(8,128)(2,1)S(1)}, bf16[1,52,52]{2,1,0:T(8,128)(2,1)}, u32[]{:S(2)}) copy-start(bf16[1,52,52]{2,1,0:T(8,128)(2,1)} %param.10) | copy-start | bytes 16228
  7.2 129.8 %all-gather.9.cloned.1.call-start = ((), (), s32[]{:S(2)}) async-start(), calls=%async_computation.4 | async-start | bytes 3932160 | tf_op jit(solution)/shard_map/all_gather | solution.py:17
  11.3 33.5 %collective-permute-start = (bf16[384,1024]{1,0:T(8,128)(2,1)}, bf16[384,1024]{1,0:T(8,128)(2,1)S(1)}, u32[]{:S(2)}, u32[]{:S(2)}) collective-permute-start(bf16[384,1024]{1,0:T(8,128)(2,1)} %bitcast.45), channel_id=1, source_target_pairs={{0,128},{1,129},{2,130},{3,131},{4,132},{5,133},{6,134},{7,135},{8... | collective-permute-start | bytes 2359304 | tf_op jit(solution)/shard_map/ppermute | solution.py:25
  38.3 6.5 %copy-start.3 = (bf16[1,384,1024]{2,1,0:T(8,128)(2,1)S(1)}, bf16[1,384,1024]{2,1,0:T(8,128)(2,1)}, u32[]{:S(2)}) copy-start(bf16[1,384,1024]{2,1,0:T(8,128)(2,1)} %param.6) | copy-start | bytes 2359300
  44.8 16.2 %copy-start.5 = (bf16[384,1024]{1,0:T(8,128)(2,1)}, bf16[384,1024]{1,0:T(8,128)(2,1)S(1)}, u32[]{:S(2)}) copy-start(bf16[384,1024]{1,0:T(8,128)(2,1)S(1)} %collective-permute-done) | copy-start | bytes 2359300
  45.8 19.6 %all-to-all-start = ((f32[16,1,384]{2,1,0:T(1,128)}), f32[16,1,384]{2,1,0:T(1,128)S(1)}, u32[]{:S(2)}, u32[]{:S(2)}) async-start(f32[16,1,384]{2,1,0:T(1,128)} %broadcast_in_dim.8), calls=%async_computation | async-start | bytes 49152 | tf_op jit(solution)/shard_map/all_to_all | solution.py:30
  65.4 0.6 copy-start.10
  65.4 6.2 %copy-start.9 = (f32[1,1024]{1,0:T(1,128)S(1)}, f32[1,1024]{1,0:T(1,128)}, u32[]{:S(2)}) copy-start(f32[1,1024]{1,0:T(1,128)} %param.9) | copy-start | bytes 12292
  66.0 70.1 %all-to-all-start.1 = ((f32[16,384,128]{1,2,0:T(8,128)}), f32[16,384,128]{1,2,0:T(8,128)S(1)}, u32[]{:S(2)}, u32[]{:S(2)}) async-start(f32[16,384,128]{1,2,0:T(8,128)} %bitcast.16), calls=%async_computation.2 | async-start | bytes 6291456 | tf_op jit(solution)/shard_map/all_to_all | solution.py:52
  70.7 70.0 %all-gather.13.cloned.1.call-start = ((), (), s32[]{:S(2)}) async-start(), calls=%async_computation.8 | async-start | bytes 3932160 | tf_op jit(solution)/shard_map/all_gather | solution.py:17
  74.2 126.3 %all-gather.11.cloned.1.call-start = ((), (), s32[]{:S(2)}) async-start(), calls=%async_computation.6 | async-start | bytes 1671168 | tf_op jit(solution)/shard_map/all_gather | solution.py:121
  136.9 127.6 %all-gather.17.cloned.1.call-start = ((), (), s32[]{:S(2)}) async-start(), calls=%async_computation.10 | async-start | bytes 3932160 | tf_op jit(solution)/shard_map/all_gather | solution.py:17
  140.6 60.0 %copy-start.8 = (bf16[384,128]{0,1:T(8,128)(2,1)S(1)}, bf16[384,128]{0,1:T(8,128)(2,1)}, u32[]{:S(2)}) copy-start(bf16[384,128]{0,1:T(8,128)(2,1)} %reduce_sum.81) | copy-start | bytes 294916
  140.7 192.8 %all-gather.15.cloned.1.call-start = ((), (), s32[]{:S(2)}) async-start(), calls=%async_computation.9 | async-start | bytes 3932160 | tf_op jit(solution)/shard_map/all_gather | solution.py:17
  144.4 235.0 %reduce-scatter.5.cloned.1.call-start = ((), (), s32[]{:S(2)}) async-start(), calls=%async_computation.7 | async-start | bytes 1179648 | tf_op jit(solution)/shard_map/reduce_scatter | solution.py:127
  203.6 63.4 %copy-start.7 = (bf16[1,384,1024]{2,1,0:T(8,128)(2,1)S(1)}, bf16[1,384,1024]{2,1,0:T(8,128)(2,1)}, u32[]{:S(2)}) copy-start(bf16[1,384,1024]{2,1,0:T(8,128)(2,1)} %param.7) | copy-start | bytes 2359300
  203.6 353.2 %reduce-scatter.3.cloned.1.call-start = ((), (), s32[]{:S(2)}) async-start(), calls=%async_computation.5 | async-start | bytes 9437184 | tf_op jit(solution)/shard_map/reduce_scatter | solution.py:58
  270.5 65.6 %copy-start.4 = (bf16[1,384,1024]{2,1,0:T(8,128)(2,1)S(1)}, bf16[1,384,1024]{2,1,0:T(8,128)(2,1)}, u32[]{:S(2)}) copy-start(bf16[1,384,1024]{2,1,0:T(8,128)(2,1)} %param.6) | copy-start | bytes 2359300
  270.5 65.6 %copy-start.6 = (bf16[384,1024]{1,0:T(8,128)(2,1)S(1)}, bf16[384,1024]{1,0:T(8,128)(2,1)}, u32[]{:S(2)}) copy-start(bf16[384,1024]{1,0:T(8,128)(2,1)} %copy-done.5) | copy-start | bytes 2359300
  336.1 2.2 copy-start.2
  342.5 216.6 %copy-start.1 = (bf16[1,52,52]{2,1,0:T(8,128)(2,1)S(1)}, bf16[1,52,52]{2,1,0:T(8,128)(2,1)}, u32[]{:S(2)}) copy-start(bf16[1,52,52]{2,1,0:T(8,128)(2,1)} %param.10) | copy-start | bytes 16228
Sparse Core Ops, SparseCore 0:
  11.4 45.8 all-gather.8
  74.4 62.6 all-gather.12
  140.1 60.3 all-gather.10
  202.2 62.1 all-gather.16
  266.1 67.3 all-gather.14
  335.9 43.5 reduce-scatter.4
  382.0 174.8 reduce-scatter.2
